TPU v7x, 256 devices: a whole 4x4x8 slice. The times are simulated.
256 devices in a mesh: dp: 8 (over x, z_hi), expert: 32 (over z_lo, y, core).
Axes of the slice: x: 4, y: 4, z: 8 (z_hi: 2, z_lo: 4; z = z_hi * 4 + z_lo), core: 2. Of those that a mesh axis runs over, the one named last changes fastest.
Arguments:
- tokens: bfloat16 [32768, 5120], P(('dp', 'expert')), may hold values from -6 to 6
- cotangent: bfloat16 [32768, 5120], P(('dp', 'expert')), may hold values from -2 to 2
- picks: int32 [256, 32, 4], P(('dp', 'expert')), may hold values from 0 to 127, as said below
- gates: float32 [256, 32, 4], P(('dp', 'expert')), may hold values from 0.05 to 1
- w_gate: bfloat16 [32, 5120, 768], P('expert', 'dp'), may hold values from -0.078125 to 0.078125
- w_up: bfloat16 [32, 5120, 768], P('expert', 'dp'), may hold values from -0.078125 to 0.078125
- w_down: bfloat16 [32, 768, 5120], P('expert', None, 'dp'), may hold values from -0.21875 to 0.21875
Outputs:
- mixed: bfloat16 [32768, 5120], P(('dp', 'expert'))
- token_grad: bfloat16 [32768, 5120], P(('dp', 'expert'))
- gate_grad: float32 [256, 32, 4], P(('dp', 'expert'))
- grad_w_gate: bfloat16 [32, 5120, 768], P('expert', 'dp')
- grad_w_up: bfloat16 [32, 5120, 768], P('expert', 'dp')
- grad_w_down: bfloat16 [32, 768, 5120], P('expert', None, 'dp')
Inputs may be any that keep to these rules, and one draw needn't show every extreme that they name: picks[d, e] holds 4 distinct token indices of device d; every expert takes exactly 4 tokens from every device.
All inputs are finite; a program needn't handle non-finite values.
Results may differ from a plain program's by a relative error of at most 0.02.
Values may be sent and summed in bfloat16 or wider, within the bound.
A program may use at most 64 MiB of HBM per device.

v0:
```python
import jax
import jax.numpy as jnp
from jax import lax
from jax.sharding import PartitionSpec as P


def contract_rows(left, right):
    return lax.dot_general(
        left, right, (((0,), (0,)), ((), ())), preferred_element_type=jnp.float32
    )


def contract_cols(left, right):
    return lax.dot_general(
        left, right, (((1,), (1,)), ((), ())), preferred_element_type=jnp.float32
    )


def rounded(values):
    return lax.optimization_barrier(values.astype(jnp.bfloat16)).astype(jnp.float32)


def swiglu_grads(column_sums, hidden_units):
    gate_sum = column_sums[:, :hidden_units]
    up_sum = column_sums[:, hidden_units : 2 * hidden_units]
    back_sum = column_sums[:, 2 * hidden_units :]
    sigmoid_gate = jax.nn.sigmoid(gate_sum)
    silu_gate = gate_sum * sigmoid_gate
    hidden = (silu_gate * up_sum).astype(jnp.bfloat16)
    grad_up = (back_sum * silu_gate).astype(jnp.bfloat16)
    grad_gate = (back_sum * up_sum * sigmoid_gate * (1.0 + gate_sum * (1.0 - sigmoid_gate))).astype(
        jnp.bfloat16
    )
    return (hidden, grad_gate, grad_up)


def body(tokens, cotangent, picks, gates, w_gate, w_up, w_down):
    expert_count = picks.shape[1]
    slot_count = picks.shape[2]
    model_width = tokens.shape[1]
    chosen = picks[0].reshape(-1)
    scales = gates[0].reshape(-1)
    token_rows = jnp.take(tokens, chosen, axis=0)
    grad_rows = jnp.take(cotangent, chosen, axis=0)
    scaled_grad = (scales[:, None] * grad_rows.astype(jnp.float32)).astype(jnp.bfloat16)
    outgoing = (
        token_rows.reshape(expert_count, slot_count, model_width),
        scaled_grad.reshape(expert_count, slot_count, model_width),
    )
    arrived_in, arrived_up = (
        lax.all_to_all(
            lax.all_to_all(outgoing[0], "dp", split_axis=2, concat_axis=1, tiled=True),
            "expert",
            split_axis=0,
            concat_axis=0,
            tiled=True,
        ),
        lax.all_to_all(
            lax.all_to_all(outgoing[1], "dp", split_axis=2, concat_axis=1, tiled=True),
            "expert",
            split_axis=0,
            concat_axis=0,
            tiled=True,
        ),
    )
    arrived_shape = arrived_in.shape
    row_count = arrived_shape[0] * arrived_shape[1]
    slice_width = arrived_shape[2]
    inputs = arrived_in.reshape(row_count, slice_width)
    upstream = arrived_up.reshape(row_count, slice_width)
    gate_mat = w_gate[0]
    up_mat = w_up[0]
    down_mat = w_down[0]
    hidden_units = gate_mat.shape[1]
    terms = jnp.concatenate(
        [
            rounded(jnp.dot(inputs, gate_mat, preferred_element_type=jnp.float32)),
            rounded(jnp.dot(inputs, up_mat, preferred_element_type=jnp.float32)),
            rounded(contract_cols(upstream, down_mat)),
        ],
        axis=1,
    )
    shares = lax.psum_scatter(
        terms.astype(jnp.bfloat16), "dp", scatter_dimension=0, tiled=True
    ).astype(jnp.float32)
    own_hidden, own_grad_gate, own_grad_up = swiglu_grads(shares, hidden_units)
    hidden, grad_gate, grad_up = (
        lax.all_gather(own_hidden, "dp", axis=0, tiled=True),
        lax.all_gather(own_grad_gate, "dp", axis=0, tiled=True),
        lax.all_gather(own_grad_up, "dp", axis=0, tiled=True),
    )
    expert_out = jnp.dot(hidden, down_mat, preferred_element_type=jnp.float32).astype(jnp.bfloat16)
    input_grad = (contract_cols(grad_gate, gate_mat) + contract_cols(grad_up, up_mat)).astype(
        jnp.bfloat16
    )
    grad_down = contract_rows(hidden, upstream).astype(jnp.bfloat16)[None]
    grad_gate_w = contract_rows(inputs, grad_gate).astype(jnp.bfloat16)[None]
    grad_up_w = contract_rows(inputs, grad_up).astype(jnp.bfloat16)[None]
    back_out, back_grad = (
        lax.all_to_all(
            lax.all_to_all(
                expert_out.reshape(arrived_shape), "dp", split_axis=1, concat_axis=2, tiled=True
            ),
            "expert",
            split_axis=0,
            concat_axis=0,
            tiled=True,
        ),
        lax.all_to_all(
            lax.all_to_all(
                input_grad.reshape(arrived_shape), "dp", split_axis=1, concat_axis=2, tiled=True
            ),
            "expert",
            split_axis=0,
            concat_axis=0,
            tiled=True,
        ),
    )
    back_out = back_out.reshape(expert_count * slot_count, model_width)
    back_grad = back_grad.reshape(expert_count * slot_count, model_width)
    positions = jnp.arange(tokens.shape[0], dtype=jnp.int32)
    select = chosen[:, None] == positions[None, :]
    weighted = jnp.where(select, scales[:, None], jnp.float32(0.0))
    out_float = back_out.astype(jnp.float32)
    mixed = lax.dot_general(
        weighted,
        out_float,
        (((0,), (0,)), ((), ())),
        precision=lax.Precision.HIGHEST,
        preferred_element_type=jnp.float32,
    ).astype(jnp.bfloat16)
    token_grad = contract_rows(select.astype(jnp.bfloat16), back_grad).astype(jnp.bfloat16)
    gate_grad = jnp.sum(grad_rows.astype(jnp.float32) * out_float, axis=1).reshape(
        1, expert_count, slot_count
    )
    return (mixed, token_grad, gate_grad, grad_gate_w, grad_up_w, grad_down)


def solution(mesh):
    return jax.shard_map(
        body,
        mesh=mesh,
        in_specs=(
            P(("dp", "expert"), None),
            P(("dp", "expert"), None),
            P(("dp", "expert"), None, None),
            P(("dp", "expert"), None, None),
            P("expert", "dp", None),
            P("expert", "dp", None),
            P("expert", None, "dp"),
        ),
        out_specs=(
            P(("dp", "expert"), None),
            P(("dp", "expert"), None),
            P(("dp", "expert"), None, None),
            P("expert", "dp", None),
            P("expert", "dp", None),
            P("expert", None, "dp"),
        ),
        check_vma=False,
    )
```

profile of v0, /device:TPU:1, one launch (start us, length us, event | category | flops | bytes accessed | tf_op | source)
XLA Modules:
  0.0 669.9 jit_solution(6501620156101534513)
XLA Ops:
  12.1 8.8 %copy.79 = bf16[32,4,5120]{0,1,2:T(4,128)(2,1)} copy(bf16[32,4,5120]{2,1,0:T(4,128)(2,1)} %reshape.48) | data formatting | bytes 2621440 | tf_op jit(solution)/shard_map/reshape | solution.py:48
  20.9 8.6 %reshape.77 = bf16[8,2,40960]{2,1,0:T(2,128)(2,1)} reshape(bf16[5120,4,32]{2,1,0:T(4,128)(2,1)} %bitcast.66) | data formatting | bytes 2621440
  29.5 11.6 %all-to-all-start.2 = ((bf16[8,2,40960]{2,1,0:T(2,128)(2,1)}), bf16[8,2,40960]{2,1,0:T(2,128)(2,1)}, u32[]{:S(2)}, u32[]{:S(2)}) async-start(bf16[8,2,40960]{2,1,0:T(2,128)(2,1)} %reshape.77), calls=%async_computation.2 | async-start | bytes 2621440 | tf_op jit(solution)/shard_map/all_to_all | solution.py:59
  41.1 2.4 gather_fusion
  43.5 1.5 broadcast_select_fusion.1
  46.3 8.8 %copy.75 = bf16[32,4,5120]{0,1,2:T(4,128)(2,1)} copy(bf16[32,4,5120]{2,1,0:T(4,128)(2,1)} %reshape.46) | data formatting | bytes 2621440 | tf_op jit(solution)/shard_map/reshape | solution.py:47
  55.1 8.7 %reshape.79 = bf16[8,2,40960]{2,1,0:T(2,128)(2,1)} reshape(bf16[5120,4,32]{2,1,0:T(4,128)(2,1)} %bitcast.67) | data formatting | bytes 2621440
  63.7 2.6 all-to-all-done.2
  66.4 6.4 all-to-all-start
  72.8 7.5 %reshape.78 = bf16[5120,4,32]{2,1,0:T(4,128)(2,1)} reshape(bf16[8,2,40960]{2,1,0:T(2,128)(2,1)} %all-to-all-done.2) | data formatting | bytes 2621440
  80.3 7.1 %copy.92 = bf16[32,4,8,640]{3,0,1,2:T(8,128)(2,1)} copy(bf16[32,4,8,640]{0,1,3,2:T(4,128)(2,1)} %bitcast.68) | data formatting | bytes 2621440 | tf_op jit(solution)/shard_map/all_to_all | solution.py:59
  87.5 2.8 copy.82
  90.2 3.4 all-to-all-done
  93.6 23.1 %all-to-all-start.3 = ((bf16[32,32,640]{2,1,0:T(8,128)(2,1)}), bf16[32,32,640]{2,1,0:T(8,128)(2,1)}, u32[]{:S(2)}, u32[]{:S(2)}) async-start(bf16[32,32,640]{2,1,0:T(8,128)(2,1)} %copy.82), calls=%async_computation.3 | async-start | bytes 2621440 | tf_op jit(solution)/shard_map/all_to_all | solution.py:58
  116.7 5.0 reshape.80
  121.7 6.0 copy.90
  129.2 19.3 %all-to-all-done.3 = bf16[32,32,640]{2,1,0:T(8,128)(2,1)} async-done(((bf16[32,32,640]{2,1,0:T(8,128)(2,1)}), bf16[32,32,640]{2,1,0:T(8,128)(2,1)}, u32[]{:S(2)}, u32[]{:S(2)}) %all-to-all-start.3) | async-done | bytes 1310752 | tf_op jit(solution)/shard_map/all_to_all | solution.py:58
  148.5 5.6 all-to-all-start.1
  154.2 4.2 convolution_convert_fusion.2
  158.4 27.5 %all-to-all-done.1 = bf16[32,32,640]{2,1,0:T(8,128)(2,1)S(1)} async-done(((bf16[32,32,640]{2,1,0:T(8,128)(2,1)}), bf16[32,32,640]{2,1,0:T(8,128)(2,1)S(1)}, u32[]{:S(2)}, u32[]{:S(2)}) %all-to-all-start.1) | async-done | bytes 1310752 | tf_op jit(solution)/shard_map/all_to_all | solution.py:51
  185.9 3.1 convolution_convert_fusion.3
  190.4 2.3 pad_maximum_fusion
  192.8 125.3 %reduce-scatter.2.cloned.1.call-done = bf16[128,2304]{1,0:T(8,128)(2,1)} async-done(((bf16[1024,2304]{1,0:T(8,128)(2,1)}), bf16[128,2304]{1,0:T(8,128)(2,1)}) %reduce-scatter.2.cloned.1.call-update) | async-done | bytes 589840 | tf_op jit(solution)/shard_map/reduce_scatter | solution.py:83
  321.6 62.8 %all-gather.4.cloned.1.call-done = bf16[1024,768]{1,0:T(8,128)(2,1)} async-done(((bf16[128,768]{1,0:T(8,128)(2,1)}), bf16[1024,768]{1,0:T(8,128)(2,1)}) %all-gather.4.cloned.1.call-update) | async-done | bytes 1572880 | tf_op jit(solution)/shard_map/all_gather | solution.py:88
  384.4 3.1 convolution_convert_fusion.5
  389.0 3.7 all-to-all-start.4
  392.6 74.9 %all-gather.6.cloned.1.call-done = bf16[1024,768]{1,0:T(8,128)(2,1)} async-done(((bf16[128,768]{1,0:T(8,128)(2,1)}), bf16[1024,768]{1,0:T(8,128)(2,1)}) %all-gather.6.cloned.1.call-update) | async-done | bytes 1572880 | tf_op jit(solution)/shard_map/all_gather | solution.py:89
  467.5 4.6 fusion.9
  472.1 63.2 %all-gather.8.cloned.1.call-done = bf16[1024,768]{1,0:T(8,128)(2,1)} async-done(((bf16[128,768]{1,0:T(8,128)(2,1)}), bf16[1024,768]{1,0:T(8,128)(2,1)}) %all-gather.8.cloned.1.call-update) | async-done | bytes 1572880 | tf_op jit(solution)/shard_map/all_gather | solution.py:90
  535.3 3.9 add_convert_fusion
  540.8 4.3 all-to-all-start.6
  545.0 1.8 copy.84
  546.8 3.6 all_to_all.77
  550.4 13.2 %all-to-all-done.6 = bf16[32,32,640]{2,0,1:T(8,128)(2,1)} async-done(((bf16[32,32,640]{2,0,1:T(8,128)(2,1)}), bf16[32,32,640]{2,0,1:T(8,128)(2,1)}, u32[]{:S(2)}, u32[]{:S(2)}) %all-to-all-start.6) | async-done | bytes 1310752 | tf_op jit(solution)/shard_map/all_to_all | solution.py:110
  563.6 25.2 %all-to-all-start.5 = ((bf16[32,4,5120]{2,1,0:T(4,128)(2,1)}), bf16[32,4,5120]{2,1,0:T(4,128)(2,1)S(1)}, u32[]{:S(2)}, u32[]{:S(2)}) async-start(bf16[32,4,5120]{2,1,0:T(4,128)(2,1)} %all_to_all.77), calls=%async_computation.6 | async-start | bytes 2621440 | tf_op jit(solution)/shard_map/all_to_all | solution.py:100
  588.8 3.1 copy.94
  591.9 3.2 all_to_all.82
  595.1 3.4 copy.87
  598.5 22.0 %all-to-all-done.5 = bf16[32,4,5120]{2,1,0:T(4,128)(2,1)S(1)} async-done(((bf16[32,4,5120]{2,1,0:T(4,128)(2,1)}), bf16[32,4,5120]{2,1,0:T(4,128)(2,1)S(1)}, u32[]{:S(2)}, u32[]{:S(2)}) %all-to-all-start.5) | async-done | bytes 1310752 | tf_op jit(solution)/shard_map/all_to_all | solution.py:100
  621.6 5.7 all-to-all-start.7
  627.3 4.3 fusion.4
  631.6 2.2 fusion.2
  633.9 2.2 fusion.3
  636.1 2.5 reshape.51
  639.9 2.4 convolution_convert_fusion.1
  642.2 16.8 %all-to-all-done.7 = bf16[32,4,5120]{2,1,0:T(4,128)(2,1)} async-done(((bf16[32,4,5120]{2,1,0:T(4,128)(2,1)}), bf16[32,4,5120]{2,1,0:T(4,128)(2,1)}, u32[]{:S(2)}, u32[]{:S(2)}) %all-to-all-start.7) | async-done | bytes 1310752 | tf_op jit(solution)/shard_map/all_to_all | solution.py:109
  659.1 2.6 reshape.53
  661.7 1.7 convolution_convert_fusion
  (49 shorter events, 18.1 us)
Async XLA Ops:
  7.2 1.9 copy-start
  29.5 11.6 %copy-start.2 = (bf16[128,5120]{1,0:T(8,128)(2,1)S(1)}, bf16[128,5120]{1,0:T(8,128)(2,1)}, u32[]{:S(2)}) copy-start(bf16[128,5120]{1,0:T(8,128)(2,1)} %param.9) | copy-start | bytes 3932164
  29.5 36.8 %all-to-all-start.2 = ((bf16[8,2,40960]{2,1,0:T(2,128)(2,1)}), bf16[8,2,40960]{2,1,0:T(2,128)(2,1)}, u32[]{:S(2)}, u32[]{:S(2)}) async-start(bf16[8,2,40960]{2,1,0:T(2,128)(2,1)} %reshape.77), calls=%async_computation.2 | async-start | bytes 2621440 | tf_op jit(solution)/shard_map/all_to_all | solution.py:59
  66.4 27.2 %all-to-all-start = ((bf16[8,2,40960]{2,1,0:T(2,128)(2,1)}), bf16[8,2,40960]{2,1,0:T(2,128)(2,1)S(1)}, u32[]{:S(2)}, u32[]{:S(2)}) async-start(bf16[8,2,40960]{2,1,0:T(2,128)(2,1)} %reshape.79), calls=%async_computation | async-start | bytes 2621440 | tf_op jit(solution)/shard_map/all_to_all | solution.py:52
  93.6 54.9 %all-to-all-start.3 = ((bf16[32,32,640]{2,1,0:T(8,128)(2,1)}), bf16[32,32,640]{2,1,0:T(8,128)(2,1)}, u32[]{:S(2)}, u32[]{:S(2)}) async-start(bf16[32,32,640]{2,1,0:T(8,128)(2,1)} %copy.82), calls=%async_computation.3 | async-start | bytes 2621440 | tf_op jit(solution)/shard_map/all_to_all | solution.py:58
  148.5 37.4 %all-to-all-start.1 = ((bf16[32,32,640]{2,1,0:T(8,128)(2,1)}), bf16[32,32,640]{2,1,0:T(8,128)(2,1)S(1)}, u32[]{:S(2)}, u32[]{:S(2)}) async-start(bf16[32,32,640]{2,1,0:T(8,128)(2,1)} %copy.78), calls=%async_computation.1 | async-start | bytes 2621440 | tf_op jit(solution)/shard_map/all_to_all | solution.py:51
  154.1 164.0 %reduce-scatter.2.cloned.1.call-start = ((), (), s32[]{:S(2)}) async-start(), calls=%async_computation.9 | async-start | bytes 5308416 | tf_op jit(solution)/shard_map/reduce_scatter | solution.py:83
  185.9 3.1 copy-start.5
  185.9 3.1 copy-start.9
  189.0 1.4 copy-start.4
  192.8 191.6 %all-gather.4.cloned.1.call-start = ((), (), s32[]{:S(2)}) async-start(), calls=%async_computation.10 | async-start | bytes 1769472 | tf_op jit(solution)/shard_map/all_gather | solution.py:88
  320.3 147.2 %all-gather.6.cloned.1.call-start = ((), (), s32[]{:S(2)}) async-start(), calls=%async_computation.11 | async-start | bytes 1769472 | tf_op jit(solution)/shard_map/all_gather | solution.py:89
  321.0 214.3 %all-gather.8.cloned.1.call-start = ((), (), s32[]{:S(2)}) async-start(), calls=%async_computation.12 | async-start | bytes 1769472 | tf_op jit(solution)/shard_map/all_gather | solution.py:90
  389.0 151.8 %all-to-all-start.4 = ((bf16[32,32,640]{2,0,1:T(8,128)(2,1)}), bf16[32,32,640]{2,0,1:T(8,128)(2,1)S(1)}, u32[]{:S(2)}, u32[]{:S(2)}) async-start(bf16[32,32,640]{2,0,1:T(8,128)(2,1)} %copy.83), calls=%async_computation.5 | async-start | bytes 2621440 | tf_op jit(solution)/shard_map/all_to_all | solution.py:101
  540.8 22.8 %all-to-all-start.6 = ((bf16[32,32,640]{2,0,1:T(8,128)(2,1)}), bf16[32,32,640]{2,0,1:T(8,128)(2,1)}, u32[]{:S(2)}, u32[]{:S(2)}) async-start(bf16[32,32,640]{2,0,1:T(8,128)(2,1)} %copy.85), calls=%async_computation.7 | async-start | bytes 2621440 | tf_op jit(solution)/shard_map/all_to_all | solution.py:110
  563.6 56.9 %all-to-all-start.5 = ((bf16[32,4,5120]{2,1,0:T(4,128)(2,1)}), bf16[32,4,5120]{2,1,0:T(4,128)(2,1)S(1)}, u32[]{:S(2)}, u32[]{:S(2)}) async-start(bf16[32,4,5120]{2,1,0:T(4,128)(2,1)} %all_to_all.77), calls=%async_computation.6 | async-start | bytes 2621440 | tf_op jit(solution)/shard_map/all_to_all | solution.py:100
  620.5 1.1 copy-start.3
  621.6 37.5 %all-to-all-start.7 = ((bf16[32,4,5120]{2,1,0:T(4,128)(2,1)}), bf16[32,4,5120]{2,1,0:T(4,128)(2,1)}, u32[]{:S(2)}, u32[]{:S(2)}) async-start(bf16[32,4,5120]{2,1,0:T(4,128)(2,1)} %copy.87), calls=%async_computation.8 | async-start | bytes 2621440 | tf_op jit(solution)/shard_map/all_to_all | solution.py:109
  627.3 4.3 copy-start.6
  627.3 4.3 copy-start.7
  631.6 2.2 copy-start.8
  659.1 4.2 copy-start.1
Sparse Core Ops, SparseCore 0:
  192.9 125.1 reduce-scatter.1
  321.3 63.1 all-gather.3
  387.6 79.8 all-gather.5
  470.5 64.7 all-gather.7
where the time goes:
time: 672 us; the launch traced here: 670 us
  waiting for transfers between devices  432 us (64%)
  local copies, waits for them, and re-layouts  97.9 us (15%)
  starting transfers between devices  85.9 us (13%)
  matrix products  33 us (5%)
  between operations  14 us (2%)
  other arithmetic  6.97 us (1%)
    reduce_scatter x1, waiting for transfers between devices, body(): lax.psum_scatter(terms.astype(jnp.bfloat16), 'dp', scatter_dimension=0, t...  125 us
    all_gather x1, waiting for transfers between devices, body(): lax.all_gather(own_grad_gate, 'dp', axis=0, tiled=True)  74.9 us
    all_gather x1, waiting for transfers between devices, body(): lax.all_gather(own_grad_up, 'dp', axis=0, tiled=True)  63.2 us
    all_gather x1, waiting for transfers between devices, body(): lax.all_gather(own_hidden, 'dp', axis=0, tiled=True)  62.8 us
    unnamed x27, local copies, waits for them, and re-layouts  33.2 us
    all_to_all x1, waiting for transfers between devices, body(): lax.all_to_all(lax.all_to_all(outgoing[0], 'dp', split_axis=2, concat_axi...  27.5 us
    all_to_all x1, starting transfers between devices, body(): lax.all_to_all(lax.all_to_all(expert_out.reshape(arrived_shape), 'dp', sp...  25.2 us
    all_to_all x1, starting transfers between devices, body(): lax.all_to_all(lax.all_to_all(outgoing[1], 'dp', split_axis=2, concat_axi...  23.1 us
  transfers between devices with their start and end apart: 12, of which 11 were waited for; matrix products, arithmetic and copies ran while one was open for 14% of the time, Pallas kernels for 0%

commit v1 on v0

--- a/solution.py
+++ b/solution.py
@@ -2,6 +2,11 @@
 import jax.numpy as jnp
 from jax import lax
 from jax.sharding import PartitionSpec as P
+
+
+def gather_over(array, mesh_axis, dim):
+    stack = jnp.stack([array] * lax.axis_size(mesh_axis))
+    return jnp.concatenate(lax.all_to_all(stack, mesh_axis, 0, 0), axis=dim)
 
 
 def contract_rows(left, right):
@@ -85,7 +90,7 @@
     ).astype(jnp.float32)
     own_hidden, own_grad_gate, own_grad_up = swiglu_grads(shares, hidden_units)
     hidden, grad_gate, grad_up = (
-        lax.all_gather(own_hidden, "dp", axis=0, tiled=True),
+        gather_over(own_hidden, "dp", 0),
         lax.all_gather(own_grad_gate, "dp", axis=0, tiled=True),
         lax.all_gather(own_grad_up, "dp", axis=0, tiled=True),
     )

time: 672 us -> 623 us (0.927)
  waiting for transfers between devices: 432 us -> 377 us
    all_gather x1 -> x0, waiting for transfers between devices: 62.8 us -> none  [body(): lax.all_gather(own_hidden, 'dp', axis=0, tiled=True)]
    all_gather x1, waiting for transfers between devices: 74.9 us -> 37 us  [body(): lax.all_gather(own_grad_gate, 'dp', axis=0, tiled=True)]
    all_to_all x0 -> x1, waiting for transfers between devices: none -> 27.3 us  [gather_over(): return jnp.concatenate(lax.all_to_all(stack, mesh_axis, 0, 0), axis=dim)]
    all_gather x1, waiting for transfers between devices: 63.2 us -> 83.1 us  [body(): lax.all_gather(own_grad_up, 'dp', axis=0, tiled=True)]
  transfers between devices with their start and end apart: 12 -> 12, of which waited for: 11 -> 11; matrix products, arithmetic and copies ran while one was open for 14% -> 15% of each run, Pallas kernels for 0% -> 0%
where the time goes in v1:
time: 623 us; the launch traced here: 620 us
  waiting for transfers between devices  377 us (61%)
  local copies, waits for them, and re-layouts  99.2 us (16%)
  starting transfers between devices  90.1 us (14%)
  matrix products  33.1 us (5%)
  between operations  14 us (2%)
  other arithmetic  6.93 us (1%)
    reduce_scatter x1, waiting for transfers between devices, body(): lax.psum_scatter(terms.astype(jnp.bfloat16), 'dp', scatter_dimension=0, t...  123 us
    all_gather x1, waiting for transfers between devices, body(): lax.all_gather(own_grad_up, 'dp', axis=0, tiled=True)  83.1 us
    all_gather x1, waiting for transfers between devices, body(): lax.all_gather(own_grad_gate, 'dp', axis=0, tiled=True)  37 us
    unnamed x27, local copies, waits for them, and re-layouts  33.3 us
    all_to_all x1, waiting for transfers between devices, body(): lax.all_to_all(lax.all_to_all(outgoing[0], 'dp', split_axis=2, concat_axi...  27.5 us
    all_to_all x1, waiting for transfers between devices, gather_over(): return jnp.concatenate(lax.all_to_all(stack, mesh_axis, 0, 0), axis=dim)  27.3 us
    all_to_all x1, starting transfers between devices, body(): lax.all_to_all(lax.all_to_all(expert_out.reshape(arrived_shape), 'dp', sp...  25.2 us
    all_to_all x1, starting transfers between devices, body(): lax.all_to_all(lax.all_to_all(outgoing[1], 'dp', split_axis=2, concat_axi...  23.1 us
  transfers between devices with their start and end apart: 12, of which 11 were waited for; matrix products, arithmetic and copies ran while one was open for 15% of the time, Pallas kernels for 0%

profile of v1, /device:TPU:1, one launch (start us, length us, event | category | flops | bytes accessed | tf_op | source)
XLA Modules:
  0.0 620.5 jit_solution(17290799600068056550)
XLA Ops:
  12.1 8.7 %copy.79 = bf16[32,4,5120]{0,1,2:T(4,128)(2,1)} copy(bf16[32,4,5120]{2,1,0:T(4,128)(2,1)} %reshape.53) | data formatting | bytes 2621440 | tf_op jit(solution)/shard_map/reshape | solution.py:53
  20.9 8.6 %reshape.83 = bf16[8,2,40960]{2,1,0:T(2,128)(2,1)} reshape(bf16[5120,4,32]{2,1,0:T(4,128)(2,1)} %bitcast.67) | data formatting | bytes 2621440
  29.5 11.6 %all-to-all-start.2 = ((bf16[8,2,40960]{2,1,0:T(2,128)(2,1)}), bf16[8,2,40960]{2,1,0:T(2,128)(2,1)}, u32[]{:S(2)}, u32[]{:S(2)}) async-start(bf16[8,2,40960]{2,1,0:T(2,128)(2,1)} %reshape.83), calls=%async_computation.2 | async-start | bytes 2621440 | tf_op jit(solution)/shard_map/all_to_all | solution.py:64
  41.1 2.4 gather_fusion
  46.3 8.7 %copy.75 = bf16[32,4,5120]{0,1,2:T(4,128)(2,1)} copy(bf16[32,4,5120]{2,1,0:T(4,128)(2,1)} %reshape.51) | data formatting | bytes 2621440 | tf_op jit(solution)/shard_map/reshape | solution.py:52
  55.1 8.7 %reshape.85 = bf16[8,2,40960]{2,1,0:T(2,128)(2,1)} reshape(bf16[5120,4,32]{2,1,0:T(4,128)(2,1)} %bitcast.68) | data formatting | bytes 2621440
  63.7 2.6 all-to-all-done.2
  66.3 6.4 %all-to-all-start = ((bf16[8,2,40960]{2,1,0:T(2,128)(2,1)}), bf16[8,2,40960]{2,1,0:T(2,128)(2,1)S(1)}, u32[]{:S(2)}, u32[]{:S(2)}) async-start(bf16[8,2,40960]{2,1,0:T(2,128)(2,1)} %reshape.85), calls=%async_computation | async-start | bytes 2621440 | tf_op jit(solution)/shard_map/all_to_all | solution.py:57
  72.8 7.5 %reshape.84 = bf16[5120,4,32]{2,1,0:T(4,128)(2,1)} reshape(bf16[8,2,40960]{2,1,0:T(2,128)(2,1)} %all-to-all-done.2) | data formatting | bytes 2621440
  80.3 7.1 %copy.92 = bf16[32,4,8,640]{3,0,1,2:T(8,128)(2,1)} copy(bf16[32,4,8,640]{0,1,3,2:T(4,128)(2,1)} %bitcast.69) | data formatting | bytes 2621440 | tf_op jit(solution)/shard_map/all_to_all | solution.py:64
  87.4 2.8 copy.82
  90.2 3.4 all-to-all-done
  93.6 23.1 %all-to-all-start.3 = ((bf16[32,32,640]{2,1,0:T(8,128)(2,1)}), bf16[32,32,640]{2,1,0:T(8,128)(2,1)}, u32[]{:S(2)}, u32[]{:S(2)}) async-start(bf16[32,32,640]{2,1,0:T(8,128)(2,1)} %copy.82), calls=%async_computation.3 | async-start | bytes 2621440 | tf_op jit(solution)/shard_map/all_to_all | solution.py:63
  116.7 5.0 reshape.86
  121.7 6.0 copy.90
  129.2 19.2 %all-to-all-done.3 = bf16[32,32,640]{2,1,0:T(8,128)(2,1)} async-done(((bf16[32,32,640]{2,1,0:T(8,128)(2,1)}), bf16[32,32,640]{2,1,0:T(8,128)(2,1)}, u32[]{:S(2)}, u32[]{:S(2)}) %all-to-all-start.3) | async-done | bytes 1310752 | tf_op jit(solution)/shard_map/all_to_all | solution.py:63
  148.5 5.6 all-to-all-start.1
  154.2 4.2 convolution_convert_fusion.2
  158.4 27.5 %all-to-all-done.1 = bf16[32,32,640]{2,1,0:T(8,128)(2,1)S(1)} async-done(((bf16[32,32,640]{2,1,0:T(8,128)(2,1)}), bf16[32,32,640]{2,1,0:T(8,128)(2,1)S(1)}, u32[]{:S(2)}, u32[]{:S(2)}) %all-to-all-start.1) | async-done | bytes 1310752 | tf_op jit(solution)/shard_map/all_to_all | solution.py:56
  185.9 3.1 convolution_convert_fusion.3
  190.4 2.3 pad_maximum_fusion
  192.8 123.5 %reduce-scatter.2.cloned.1.call-done = bf16[128,2304]{1,0:T(8,128)(2,1)} async-done(((bf16[1024,2304]{1,0:T(8,128)(2,1)}), bf16[128,2304]{1,0:T(8,128)(2,1)}) %reduce-scatter.2.cloned.1.call-update) | async-done | bytes 589840 | tf_op jit(solution)/shard_map/reduce_scatter | solution.py:88
  319.8 4.5 all-to-all-start.4
  325.0 27.3 %all-to-all-done.4 = bf16[8,128,768]{2,1,0:T(8,128)(2,1)} async-done(((bf16[8,128,768]{2,1,0:T(8,128)(2,1)}), bf16[8,128,768]{2,1,0:T(8,128)(2,1)}, u32[]{:S(2)}, u32[]{:S(2)}) %all-to-all-start.4) | async-done | bytes 1572896 | tf_op jit(solution)/shard_map/all_to_all | solution.py:9
  352.3 3.1 convolution_convert_fusion.5
  356.9 3.6 all-to-all-start.5
  360.4 37.0 %all-gather.3.cloned.1.call-done = bf16[1024,768]{1,0:T(8,128)(2,1)} async-done(((bf16[128,768]{1,0:T(8,128)(2,1)}), bf16[1024,768]{1,0:T(8,128)(2,1)}) %all-gather.3.cloned.1.call-update) | async-done | bytes 1572880 | tf_op jit(solution)/shard_map/all_gather | solution.py:94
  397.4 4.6 fusion.9
  402.0 83.1 %all-gather.5.cloned.1.call-done = bf16[1024,768]{1,0:T(8,128)(2,1)} async-done(((bf16[128,768]{1,0:T(8,128)(2,1)}), bf16[1024,768]{1,0:T(8,128)(2,1)}) %all-gather.5.cloned.1.call-update) | async-done | bytes 1572880 | tf_op jit(solution)/shard_map/all_gather | solution.py:95
  485.2 3.9 add_convert_fusion
  490.6 4.3 all-to-all-start.7
  494.9 1.8 copy.84
  496.7 3.6 all_to_all.81
  500.3 13.2 %all-to-all-done.7 = bf16[32,32,640]{2,0,1:T(8,128)(2,1)} async-done(((bf16[32,32,640]{2,0,1:T(8,128)(2,1)}), bf16[32,32,640]{2,0,1:T(8,128)(2,1)}, u32[]{:S(2)}, u32[]{:S(2)}) %all-to-all-start.7) | async-done | bytes 1310752 | tf_op jit(solution)/shard_map/all_to_all | solution.py:115
  513.4 25.2 %all-to-all-start.6 = ((bf16[32,4,5120]{2,1,0:T(4,128)(2,1)}), bf16[32,4,5120]{2,1,0:T(4,128)(2,1)S(1)}, u32[]{:S(2)}, u32[]{:S(2)}) async-start(bf16[32,4,5120]{2,1,0:T(4,128)(2,1)} %all_to_all.81), calls=%async_computation.7 | async-start | bytes 2621440 | tf_op jit(solution)/shard_map/all_to_all | solution.py:105
  538.6 3.1 copy.94
  541.7 3.2 all_to_all.86
  545.0 3.4 copy.87
  548.4 22.0 %all-to-all-done.6 = bf16[32,4,5120]{2,1,0:T(4,128)(2,1)S(1)} async-done(((bf16[32,4,5120]{2,1,0:T(4,128)(2,1)}), bf16[32,4,5120]{2,1,0:T(4,128)(2,1)S(1)}, u32[]{:S(2)}, u32[]{:S(2)}) %all-to-all-start.6) | async-done | bytes 1310752 | tf_op jit(solution)/shard_map/all_to_all | solution.py:105
  571.4 5.7 all-to-all-start.8
  577.2 4.3 fusion.4
  581.5 2.2 fusion.2
  583.7 2.2 fusion.3
  585.9 2.5 reshape.57
  589.0 2.4 convolution_convert_fusion.1
  591.3 17.6 %all-to-all-done.8 = bf16[32,4,5120]{2,1,0:T(4,128)(2,1)} async-done(((bf16[32,4,5120]{2,1,0:T(4,128)(2,1)}), bf16[32,4,5120]{2,1,0:T(4,128)(2,1)}, u32[]{:S(2)}, u32[]{:S(2)}) %all-to-all-start.8) | async-done | bytes 1310752 | tf_op jit(solution)/shard_map/all_to_all | solution.py:114
  608.9 2.6 reshape.59
  611.5 1.7 convolution_convert_fusion
  (49 shorter events, 20.2 us)
Async XLA Ops:
  7.2 1.9 copy-start
  29.5 11.6 %copy-start.2 = (bf16[128,5120]{1,0:T(8,128)(2,1)S(1)}, bf16[128,5120]{1,0:T(8,128)(2,1)}, u32[]{:S(2)}) copy-start(bf16[128,5120]{1,0:T(8,128)(2,1)} %param.9) | copy-start | bytes 3932164
  29.5 36.8 %all-to-all-start.2 = ((bf16[8,2,40960]{2,1,0:T(2,128)(2,1)}), bf16[8,2,40960]{2,1,0:T(2,128)(2,1)}, u32[]{:S(2)}, u32[]{:S(2)}) async-start(bf16[8,2,40960]{2,1,0:T(2,128)(2,1)} %reshape.83), calls=%async_computation.2 | async-start | bytes 2621440 | tf_op jit(solution)/shard_map/all_to_all | solution.py:64
  66.3 27.2 %all-to-all-start = ((bf16[8,2,40960]{2,1,0:T(2,128)(2,1)}), bf16[8,2,40960]{2,1,0:T(2,128)(2,1)S(1)}, u32[]{:S(2)}, u32[]{:S(2)}) async-start(bf16[8,2,40960]{2,1,0:T(2,128)(2,1)} %reshape.85), calls=%async_computation | async-start | bytes 2621440 | tf_op jit(solution)/shard_map/all_to_all | solution.py:57
  93.6 54.9 %all-to-all-start.3 = ((bf16[32,32,640]{2,1,0:T(8,128)(2,1)}), bf16[32,32,640]{2,1,0:T(8,128)(2,1)}, u32[]{:S(2)}, u32[]{:S(2)}) async-start(bf16[32,32,640]{2,1,0:T(8,128)(2,1)} %copy.82), calls=%async_computation.3 | async-start | bytes 2621440 | tf_op jit(solution)/shard_map/all_to_all | solution.py:63
  148.5 37.4 %all-to-all-start.1 = ((bf16[32,32,640]{2,1,0:T(8,128)(2,1)}), bf16[32,32,640]{2,1,0:T(8,128)(2,1)S(1)}, u32[]{:S(2)}, u32[]{:S(2)}) async-start(bf16[32,32,640]{2,1,0:T(8,128)(2,1)} %copy.78), calls=%async_computation.1 | async-start | bytes 2621440 | tf_op jit(solution)/shard_map/all_to_all | solution.py:56
  154.1 162.2 %reduce-scatter.2.cloned.1.call-start = ((), (), s32[]{:S(2)}) async-start(), calls=%async_computation.10 | async-start | bytes 5308416 | tf_op jit(solution)/shard_map/reduce_scatter | solution.py:88
  185.9 3.1 copy-start.5
  185.9 3.1 copy-start.9
  189.0 1.4 copy-start.4
  192.8 204.7 %all-gather.3.cloned.1.call-start = ((), (), s32[]{:S(2)}) async-start(), calls=%async_computation.11 | async-start | bytes 1769472 | tf_op jit(solution)/shard_map/all_gather | solution.py:94
  319.8 32.6 %all-to-all-start.4 = ((bf16[8,128,768]{2,1,0:T(8,128)(2,1)}), bf16[8,128,768]{2,1,0:T(8,128)(2,1)}, u32[]{:S(2)}, u32[]{:S(2)}) async-start(bf16[8,128,768]{2,1,0:T(8,128)(2,1)} %stack.2), calls=%async_computation.5 | async-start | bytes 3145728 | tf_op jit(solution)/shard_map/all_to_all | solution.py:9
  324.2 160.9 %all-gather.5.cloned.1.call-start = ((), (), s32[]{:S(2)}) async-start(), calls=%async_computation.12 | async-start | bytes 1769472 | tf_op jit(solution)/shard_map/all_gather | solution.py:95
  356.9 133.8 %all-to-all-start.5 = ((bf16[32,32,640]{2,0,1:T(8,128)(2,1)}), bf16[32,32,640]{2,0,1:T(8,128)(2,1)S(1)}, u32[]{:S(2)}, u32[]{:S(2)}) async-start(bf16[32,32,640]{2,0,1:T(8,128)(2,1)} %copy.83), calls=%async_computation.6 | async-start | bytes 2621440 | tf_op jit(solution)/shard_map/all_to_all | solution.py:106
  490.6 22.8 %all-to-all-start.7 = ((bf16[32,32,640]{2,0,1:T(8,128)(2,1)}), bf16[32,32,640]{2,0,1:T(8,128)(2,1)}, u32[]{:S(2)}, u32[]{:S(2)}) async-start(bf16[32,32,640]{2,0,1:T(8,128)(2,1)} %copy.85), calls=%async_computation.8 | async-start | bytes 2621440 | tf_op jit(solution)/shard_map/all_to_all | solution.py:115
  513.4 56.9 %all-to-all-start.6 = ((bf16[32,4,5120]{2,1,0:T(4,128)(2,1)}), bf16[32,4,5120]{2,1,0:T(4,128)(2,1)S(1)}, u32[]{:S(2)}, u32[]{:S(2)}) async-start(bf16[32,4,5120]{2,1,0:T(4,128)(2,1)} %all_to_all.81), calls=%async_computation.7 | async-start | bytes 2621440 | tf_op jit(solution)/shard_map/all_to_all | solution.py:105
  570.4 1.1 copy-start.3
  571.4 37.5 %all-to-all-start.8 = ((bf16[32,4,5120]{2,1,0:T(4,128)(2,1)}), bf16[32,4,5120]{2,1,0:T(4,128)(2,1)}, u32[]{:S(2)}, u32[]{:S(2)}) async-start(bf16[32,4,5120]{2,1,0:T(4,128)(2,1)} %copy.87), calls=%async_computation.9 | async-start | bytes 2621440 | tf_op jit(solution)/shard_map/all_to_all | solution.py:114
  577.1 4.3 copy-start.6
  577.1 4.3 copy-start.7
  581.5 2.2 copy-start.8
  608.9 5.0 copy-start.1
Sparse Core Ops, SparseCore 0:
  192.9 123.3 reduce-scatter.1
  319.5 77.8 all-gather.2
  400.6 84.5 all-gather.4
